TPU v7x, 32 devices: a whole 2x2x4 slice. The times are simulated.
32 devices in a mesh: groups: 2 (over y), rows: 4 (over x, core), cents: 4 (over z).
Axes of the slice: x: 2, y: 2, z: 4, core: 2. Of those that a mesh axis runs over, the one named last changes fastest.
Arguments:
- embedding: bfloat16 [2048, 128], P(('groups', 'rows', 'cents')), parts along dimension 0, may hold values from -8 to 8
- degrees: int32 [2048], P(('groups', 'rows', 'cents')), parts along dimension 0, may hold values from 1 to 63
- rotation: float32 [128, 128], replicated, may hold values from -0.5 to 0.5
- offsets: float32 [8192, 128], P(('groups', 'cents')), parts along dimension 0, may hold values from -2 to 2
- seed_ids: int32 [8192], P(('groups', 'cents')), parts along dimension 0, may hold values from 0 to 1023
Outputs:
- energy: float32 [2048], P(('groups', 'rows', 'cents')), parts along dimension 0
- centroids: float32 [8192, 128], P(('groups', 'cents')), parts along dimension 0
There are 2 independent parts, one for each index of `groups`. A program takes and returns all parts, laid end to end along the dimension named above; an argument that names none is the same for every part. Nothing has to cross between parts.
All inputs are finite; a program needn't handle non-finite values.
Results may differ from a plain program's by a relative error of at most 0.024.
Values may be sent and summed in bfloat16 or wider, within the bound.
A program may use at most 64 MiB of HBM per device.

v0:
```python
import jax
import jax.numpy as jnp
from jax import lax
from jax.sharding import PartitionSpec as P

ITERS = 2


sharpness_scale = 0.1
ridge = 0.01


def lower_factor(matrix):
    width = matrix.shape[0]
    positions = jnp.arange(width, dtype=jnp.int32)

    def column_step(index, factor):
        row_here = lax.dynamic_index_in_dim(factor, index, 0, keepdims=False)
        column = lax.dynamic_index_in_dim(matrix, index, 1, keepdims=False)
        column = column - jnp.dot(factor, row_here, precision=lax.Precision.HIGHEST)
        pivot = jnp.sqrt(lax.dynamic_index_in_dim(column, index, 0, keepdims=False))
        column = jnp.where(positions > index, column / pivot, jnp.zeros((), column.dtype))
        column = jnp.where(positions == index, pivot, column)
        return lax.dynamic_update_slice_in_dim(factor, column[:, None], index, 1)

    return lax.fori_loop(0, width, column_step, jnp.zeros(matrix.shape, matrix.dtype))


def upper_solve(factor, target):
    width = factor.shape[0]

    def row_step(count, solved):
        index = width - 1 - count
        column = lax.dynamic_index_in_dim(factor, index, 1, keepdims=False)
        pivot = lax.dynamic_index_in_dim(column, index, 0, keepdims=False)
        target_row = lax.dynamic_index_in_dim(target, index, 0, keepdims=False)
        value = (target_row - jnp.dot(column, solved, precision=lax.Precision.HIGHEST)) / pivot
        return lax.dynamic_update_slice_in_dim(solved, value[None, :], index, 0)

    return lax.fori_loop(0, width, row_step, jnp.zeros(target.shape, target.dtype))


def block_affinity_logits(rows_block, piece_entry_lengths, cent_bf, mean_point_sqlength):
    pairwise_dots = lax.dot_general(
        rows_block, cent_bf, (((1,), (1,)), ((), ())), preferred_element_type=jnp.float32
    )
    return (
        2.0 * pairwise_dots - mean_point_sqlength[None, :] - piece_entry_lengths[:, None]
    ) / sharpness_scale


def shards(embedding, degrees, rotation, offsets, seed_ids):
    local_entries = embedding.shape[0]
    width = embedding.shape[1]
    total_rows = local_entries * lax.axis_size("rows") * lax.axis_size("cents")
    partial_gram_matrix = lax.dot_general(
        embedding, embedding, (((0,), (0,)), ((), ())), preferred_element_type=jnp.float32
    )
    gram = lax.psum(partial_gram_matrix, ("rows", "cents"))
    shifted = gram / total_rows + ridge * jnp.eye(width, dtype=jnp.float32)
    cholesky_lower_factor = lower_factor(shifted)
    turned = upper_solve(cholesky_lower_factor, rotation).astype(jnp.bfloat16)
    mixed = jnp.dot(embedding, turned, preferred_element_type=jnp.float32)
    unit = (mixed * lax.rsqrt(jnp.sum(mixed * mixed, axis=1, keepdims=True) + 1e-06)).astype(
        jnp.bfloat16
    )
    gathered, degree_rows = (
        lax.all_gather(unit, "cents", axis=0, tiled=True),
        lax.all_gather(degrees.astype(jnp.bfloat16), "cents", axis=0, tiled=True),
    )
    count = gathered.shape[0]
    weights = jnp.sqrt(degree_rows.astype(jnp.float32))
    sq_norms = jnp.sum(jnp.square(gathered.astype(jnp.float32)), axis=1)
    local_ids = seed_ids - lax.axis_index("rows") * count
    block_rows = min(512, count)
    block_count = count // block_rows
    rows_blocks = gathered.reshape(block_count, block_rows, width)
    norm_blocks = sq_norms.reshape(block_count, block_rows)
    weight_blocks = weights.reshape(block_count, block_rows)
    block_starts = jnp.arange(block_count, dtype=jnp.int32) * block_rows
    row_positions = jnp.arange(block_rows, dtype=jnp.int32)

    def seed_block(carry, pack):
        selector = ((local_ids - pack[1])[:, None] == row_positions[None, :]).astype(jnp.bfloat16)
        return (carry + jnp.dot(selector, pack[0], preferred_element_type=jnp.float32), None)

    picked_sum, unused_seed = lax.scan(
        seed_block, jnp.zeros((seed_ids.shape[0], width), jnp.float32), (rows_blocks, block_starts)
    )
    picked = picked_sum.astype(jnp.bfloat16)
    centers = lax.psum(picked, "rows").astype(jnp.float32) + offsets
    energy = jnp.zeros((count,), jnp.float32)
    for step in range(ITERS):
        cent_bf = centers.astype(jnp.bfloat16)
        mean_point_sqlength = jnp.sum(centers * centers, axis=1)

        def local_stats(pack):
            logits = block_affinity_logits(pack[0], pack[1], cent_bf, mean_point_sqlength)
            peak = jnp.max(logits, axis=1)
            return (peak, jnp.sum(jnp.exp(logits - peak[:, None]), axis=1))

        peaks, totals = lax.map(local_stats, (rows_blocks, norm_blocks))
        larger = lax.pmax(peaks, "cents")
        whole = lax.psum(totals * jnp.exp(peaks - larger), "cents")

        def accumulate(carry, pack):
            logits = block_affinity_logits(pack[0], pack[1], cent_bf, mean_point_sqlength)
            probs = jnp.exp(logits - pack[2][:, None]) / pack[3][:, None]
            shares = (pack[4][:, None] * probs).astype(jnp.bfloat16)
            moved = lax.dot_general(
                shares, pack[0], (((0,), (0,)), ((), ())), preferred_element_type=jnp.float32
            )
            return (
                (carry[0] + moved, carry[1] + jnp.sum(shares.astype(jnp.float32), axis=0)),
                None,
            )

        start = (jnp.zeros(centers.shape, jnp.float32), jnp.zeros((centers.shape[0],), jnp.float32))
        (sums, masses), unused = lax.scan(
            accumulate, start, (rows_blocks, norm_blocks, larger, whole, weight_blocks)
        )
        energy = (larger + jnp.log(whole)).reshape(count)
        full_sums, full_masses = (
            lax.psum(sums.astype(jnp.bfloat16), "rows").astype(jnp.float32),
            lax.psum(masses.astype(jnp.bfloat16), "rows").astype(jnp.float32),
        )
        centers = (full_sums + centers) / (full_masses + 1.0)[:, None]
    own_energy = lax.dynamic_slice_in_dim(
        energy, lax.axis_index("cents") * local_entries, local_entries
    )
    return (own_energy, centers)


def solution(mesh):
    placed = (
        P(("groups", "rows", "cents"), None),
        P(("groups", "rows", "cents")),
        P(),
        P(("groups", "cents"), None),
        P(("groups", "cents")),
    )
    return jax.shard_map(
        shards,
        mesh=mesh,
        in_specs=placed,
        out_specs=(P(("groups", "rows", "cents")), P(("groups", "cents"), None)),
        check_vma=False,
    )
```

profile of v0, /device:TPU:0, one launch (start us, length us, event | category | flops | bytes accessed | tf_op | source)
XLA Modules:
  0.0 808.0 jit_solution(4638034713147383374)
XLA Ops:
  12.3 13.4 %all-reduce = bf16[256]{0:T(256)(128)(2,1)S(1)} all-reduce(bf16[256]{0:T(256)(128)(2,1)S(1)} %dynamic-update-slice), channel_id=1, replica_groups=mesh['groups'=2,'rows'=4,'cents'=4] {'cents'}, use_global_device_ids=true, to_apply=%add | all-reduce | flops 256 | bytes 1024
  25.7 73.5 %all-reduce.6.cloned.1.call-done = f32[128,128]{0,1:T(8,128)} async-done(((f32[128,128]{0,1:T(8,128)}), f32[128,128]{0,1:T(8,128)}) %all-reduce.6.cloned.1.call-update) | async-done | bytes 65552 | tf_op jit(solution)/shard_map/psum | solution.py:59
  100.1 257.5 %while.22 = (s32[]{:T(128)}, f32[128,128]{1,0:T(8,128)S(1)}, f32[128,128]{0,1:T(8,128)S(1)}, s32[]{:T(128)}, s32[]{:T(128)}) while((s32[]{:T(128)}, f32[128,128]{1,0:T(8,128)S(1)}, f32[128,128]{0,1:T(8,128)S(1)}, s32[]{:T(128)}, s32[]{:T(128)}) %tuple.89), condition=%wide.region_2.3_spmd.clone.clone, body=%wide.region_1.2_spmd.clone.clone.sunk | while | flops 197378 | bytes 71269 | solution.py:26
  357.6 273.3 %while.21 = (s32[]{:T(128)}, f32[128,128]{1,0:T(8,128)S(1)}, f32[128,128]{1,0:T(8,128)}, f32[128,128]{0,1:T(8,128)S(1)}, s32[]{:T(128)}, /*index=5*/s32[]{:T(128)}, s32[]{:T(128)}, s32[]{:T(128)}) while((s32[]{:T(128)}, f32[128,128]{1,0:T(8,128)S(1)}, f32[128,128]{1,0:T(8,128)}, f32[128,128]{0,1:T(8,128)S(1)}, s32[]{:T(128)}, ...), condition=%wide.region_4.5_spmd, body=%wide.region_3.4_spmd.sunk | while | flops 196871 | bytes 69295 | solution.py:40
  358.2 1.5 fusion.51
  360.4 1.5 fusion.51
  362.5 1.5 fusion.51
  364.7 1.5 fusion.51
  366.8 1.5 fusion.51
  368.9 1.5 fusion.51
  371.1 1.5 fusion.51
  373.2 1.5 fusion.51
  392.4 1.5 fusion.51
  394.6 1.5 fusion.51
  396.7 1.5 fusion.51
  398.8 1.5 fusion.51
  401.0 1.5 fusion.51
  403.1 1.5 fusion.51
  405.2 1.5 fusion.51
  407.4 1.5 fusion.51
  426.6 1.5 fusion.51
  428.7 1.5 fusion.51
  430.9 1.5 fusion.51
  433.0 1.5 fusion.51
  435.1 1.5 fusion.51
  437.3 1.5 fusion.51
  439.4 1.5 fusion.51
  441.5 1.5 fusion.51
  460.8 1.5 fusion.51
  462.9 1.5 fusion.51
  465.0 1.5 fusion.51
  467.2 1.5 fusion.51
  469.3 1.5 fusion.51
  471.4 1.5 fusion.51
  473.6 1.5 fusion.51
  475.7 1.5 fusion.51
  494.9 1.5 fusion.51
  497.1 1.5 fusion.51
  499.2 1.5 fusion.51
  501.3 1.5 fusion.51
  503.5 1.5 fusion.51
  505.6 1.5 fusion.51
  507.7 1.5 fusion.51
  509.9 1.5 fusion.51
  529.1 1.5 fusion.51
  531.2 1.5 fusion.51
  533.4 1.5 fusion.51
  537.6 1.5 fusion.51
  541.9 1.5 fusion.51
  565.4 1.5 fusion.51
  576.1 1.5 fusion.51
  599.6 1.5 fusion.51
  603.8 1.5 fusion.51
  631.3 14.2 %all_gather.6 = bf16[256,128]{1,0:T(8,128)(2,1)S(1)} all-gather(bf16[64,128]{1,0:T(8,128)(2,1)S(1)} %fusion.23), channel_id=1, replica_groups=mesh['groups'=2,'rows'=4,'cents'=4] {'cents'}, dimensions={0}, use_global_device_ids=true | all-gather | bytes 81920 | tf_op jit(solution)/shard_map/all_gather | solution.py:68
  646.8 32.5 %all-reduce.8.cloned.1.call-done = bf16[1024,128]{1,0:T(8,128)(2,1)} async-done(((bf16[1024,128]{1,0:T(8,128)(2,1)}), bf16[1024,128]{1,0:T(8,128)(2,1)}) %all-reduce.8.cloned.1.call-update) | async-done | bytes 262160 | tf_op jit(solution)/shard_map/psum | solution.py:91
  681.0 11.7 %pmax.14 = f32[1,256]{1,0:T(1,128)S(1)} all-reduce(f32[1,256]{1,0:T(1,128)S(1)} %bitcast.76), channel_id=1, replica_groups=mesh['groups'=2,'rows'=4,'cents'=4] {'cents'}, use_global_device_ids=true, to_apply=%region_10.11 | all-reduce | flops 256 | bytes 2048 | tf_op jit(solution)/shard_map/pmax | solution.py:103
  693.0 8.4 %psum.58 = f32[256]{0:T(256)S(1)} all-reduce(f32[256]{0:T(256)S(1)} %bitcast.81), channel_id=1, replica_groups=mesh['groups'=2,'rows'=4,'cents'=4] {'cents'}, use_global_device_ids=true, to_apply=%region_12.13 | all-reduce | flops 256 | bytes 2048 | tf_op jit(solution)/shard_map/psum | solution.py:104
  701.7 5.8 psum.60
  708.6 30.8 %all-reduce.10.cloned.1.call-done = bf16[1024,128]{1,0:T(8,128)(2,1)} async-done(((bf16[1024,128]{1,0:T(8,128)(2,1)}), bf16[1024,128]{1,0:T(8,128)(2,1)}) %all-reduce.10.cloned.1.call-update) | async-done | bytes 262160 | tf_op jit(solution)/shard_map/psum | solution.py:124
  741.1 11.7 %pmax.15 = f32[1,256]{1,0:T(1,128)S(1)} all-reduce(f32[1,256]{1,0:T(1,128)S(1)} %bitcast.74), channel_id=1, replica_groups=mesh['groups'=2,'rows'=4,'cents'=4] {'cents'}, use_global_device_ids=true, to_apply=%region_18.19 | all-reduce | flops 256 | bytes 2048 | tf_op jit(solution)/shard_map/pmax | solution.py:103
  753.1 8.4 %psum.61 = f32[1,256]{1,0:T(1,128)S(1)} all-reduce(f32[1,256]{1,0:T(1,128)S(1)} %exponential_multiply_fusion), channel_id=1, replica_groups=mesh['groups'=2,'rows'=4,'cents'=4] {'cents'}, use_global_device_ids=true, to_apply=%region_20.21 | all-reduce | flops 256 | bytes 2048 | tf_op jit(solution)/shard_map/psum | solution.py:104
  761.8 5.8 psum.63
  769.3 30.2 %all-reduce.12.cloned.1.call-done = bf16[1024,128]{1,0:T(8,128)(2,1)} async-done(((bf16[1024,128]{1,0:T(8,128)(2,1)}), bf16[1024,128]{1,0:T(8,128)(2,1)}) %all-reduce.12.cloned.1.call-update) | async-done | bytes 262160 | tf_op jit(solution)/shard_map/psum | solution.py:124
  799.5 1.9 add_divide_fusion
  (1026 shorter events, 375.9 us)
Async XLA Ops:
  7.2 0.7 copy-start
  7.2 92.0 %all-reduce.6.cloned.1.call-start = ((), (), s32[]{:S(2)}) async-start(), calls=%async_computation | async-start | bytes 131072 | tf_op jit(solution)/shard_map/psum | solution.py:59
  8.8 670.5 %all-reduce.8.cloned.1.call-start = ((), (), s32[]{:S(2)}) async-start(), calls=%async_computation.1 | async-start | bytes 524288 | tf_op jit(solution)/shard_map/psum | solution.py:91
  8.8 0.7 copy-start.3
  9.5 0.7 copy-start.4
  10.2 0.7 copy-start.5
  631.0 48.3 %copy-start.1 = (f32[1024,128]{1,0:T(8,128)S(1)}, f32[1024,128]{1,0:T(8,128)}, u32[]{:S(2)}) copy-start(f32[1024,128]{1,0:T(8,128)} %param.12) | copy-start | bytes 1572868
  646.6 92.7 %all-reduce.10.cloned.1.call-start = ((), (), s32[]{:S(2)}) async-start(), calls=%async_computation.2 | async-start | bytes 524288 | tf_op jit(solution)/shard_map/psum | solution.py:124
  679.3 1.2 copy-start.2
  708.6 91.0 %all-reduce.12.cloned.1.call-start = ((), (), s32[]{:S(2)}) async-start(), calls=%async_computation.3 | async-start | bytes 524288 | tf_op jit(solution)/shard_map/psum | solution.py:124
Sparse Core Ops, SparseCore 0:
  12.0 87.1 all-reduce.5
  646.8 32.4 all-reduce.7
  708.7 30.6 all-reduce.9
  768.8 30.6 all-reduce.11
where the time goes:
time: 815 us; the launch traced here: 808 us
  local copies, waits for them, and re-layouts  225 us (28%)
  matrix products  218 us (27%)
  waiting for transfers between devices  167 us (20%)
  loops' own time  96.5 us (12%)
  blocking collectives  79.4 us (10%)
  between operations  14.6 us (2%)
  other arithmetic  8.24 us (1%)
    dot_general x128, matrix products, row_step(): jnp.dot(column, solved, precision=lax.Precision.HIGHEST)  190 us
    another operation x1, loops' own time, lower_factor(): lax.fori_loop(0, width, column_step, jnp.zeros(matrix.shape, matrix.dtype))  92.7 us
    dynamic_slice x128, local copies, waits for them, and re-layouts, column_step(): pivot = jnp.sqrt(lax.dynamic_index_in_dim(column, index, 0, keepdims=False))  81.4 us
    dynamic_slice x128, local copies, waits for them, and re-layouts, row_step(): pivot = lax.dynamic_index_in_dim(column, index, 0, keepdims=False)  75.3 us
    psum x1, waiting for transfers between devices, shards(): gram = lax.psum(partial_gram_matrix, ('rows', 'cents'))  73.5 us
    psum x2, waiting for transfers between devices, shards(): lax.psum(sums.astype(jnp.bfloat16), 'rows').astype(jnp.float32)  60.9 us
    dynamic_update_slice x128, local copies, waits for them, and re-layouts, column_step(): return lax.dynamic_update_slice_in_dim(factor, column[:, None], index, 1)  45.9 us
    psum x1, waiting for transfers between devices, shards(): centers = lax.psum(picked, 'rows').astype(jnp.float32) + offsets  32.5 us
  transfers between devices with their start and end apart: 4, of which 4 were waited for; matrix products, arithmetic and copies ran while one was open for 0% of the time, Pallas kernels for 0%

commit v1 on v0

--- a/solution.py
+++ b/solution.py
@@ -1,6 +1,11 @@
+import functools
+import math
+
 import jax
 import jax.numpy as jnp
 from jax import lax
+from jax.experimental import pallas as pl
+from jax.experimental.pallas import tpu as pltpu
 from jax.sharding import PartitionSpec as P
 
 ITERS = 2
@@ -131,7 +136,262 @@
     return (own_energy, centers)
 
 
+MESH = pl.DeviceIdType.MESH
+LOG2E = math.log2(math.e)
+LN2 = math.log(2.0)
+GATHER_ROWS = 2048
+BLOCK = 8
+
+
+def vmem(count):
+    return [pl.BlockSpec(memory_space=pltpu.VMEM)] * count
+
+
+def gather_kernel(n_rows, n_cents, emb_ref, deg_ref, all_ref, weight_ref, shifted_ref, held, send_sem, recv_sem):
+    group = lax.axis_index("groups")
+    me = lax.axis_index("rows") * n_cents + lax.axis_index("cents")
+    members = n_rows * n_cents
+    local, width = emb_ref.shape
+
+    def peer(step):
+        other = lax.rem(me + step, members)
+        return (group, other // n_cents, lax.rem(other, n_cents))
+
+    barrier = pltpu.get_barrier_semaphore()
+    for step in range(1, members):
+        pl.semaphore_signal(barrier, inc=1, device_id=peer(step), device_id_type=MESH)
+    held[me, :local, :] = emb_ref[...]
+    tag = jnp.concatenate(
+        [deg_ref[...].astype(jnp.float32), jnp.zeros((1, width - local), jnp.float32)], axis=1
+    )
+    held[me, local:, :] = jnp.broadcast_to(tag, (16, width)).astype(jnp.bfloat16)
+    pl.semaphore_wait(barrier, members - 1)
+    copies = []
+    for step in range(1, members):
+        copy = pltpu.make_async_remote_copy(
+            src_ref=held.at[me],
+            dst_ref=held.at[me],
+            send_sem=send_sem.at[step - 1],
+            recv_sem=recv_sem.at[step - 1],
+            device_id=peer(step),
+            device_id_type=MESH,
+        )
+        copy.start()
+        copies.append(copy)
+    for copy in copies:
+        copy.wait()
+    rows = held[:, :local, :].reshape(members * local, width)
+    all_ref[...] = rows
+    gram = lax.dot_general(rows, rows, (((0,), (0,)), ((), ())), preferred_element_type=jnp.float32)
+    eye = lax.broadcasted_iota(jnp.int32, gram.shape, 0) == lax.broadcasted_iota(jnp.int32, gram.shape, 1)
+    shifted_ref[...] = gram / (members * local) + jnp.where(eye, ridge, 0.0)
+    tags = held[:, local:, :].astype(jnp.float32)
+    weight_ref[...] = jnp.sqrt(
+        jnp.concatenate([tags[index, :1, :local] for index in range(members)], axis=1)
+    )
+
+
+def factor_kernel(matrix_ref, rotation_ref, turned_ref):
+    width = matrix_ref.shape[0]
+    left = matrix_ref[...]
+    row_id = lax.broadcasted_iota(jnp.int32, (width, width), 0)
+    col_id = lax.broadcasted_iota(jnp.int32, (width, width), 1)
+    right = jnp.where(row_id == col_id, 1.0, 0.0).astype(jnp.float32)
+    both = jnp.concatenate([left, right], axis=1)
+    sub = lax.broadcasted_iota(jnp.int32, (BLOCK, width), 0)
+    solved = []
+    for block in range(width // BLOCK):
+        at = block * BLOCK
+        a = both[at : at + BLOCK, :width]
+        v = both[at : at + BLOCK, width:]
+        columns = [jnp.broadcast_to(a[:, at + j : at + j + 1], (BLOCK, width)) for j in range(BLOCK)]
+        pivots = jnp.ones((BLOCK, width), jnp.float32)
+        for j in range(BLOCK):
+            pivot = columns[j][j : j + 1, :]
+            inverse = 1.0 / pivot
+            pivots = jnp.where(sub == j, pivot, pivots)
+            share = jnp.where(sub > j, columns[j] * inverse, 0.0)
+            for l in range(j + 1, BLOCK):
+                columns[l] = columns[l] - share * columns[l][j : j + 1, :]
+            a = a - share * a[j : j + 1, :]
+            v = v - share * v[j : j + 1, :]
+        solved.append(v * lax.rsqrt(pivots))
+        if at + BLOCK < width:
+            both = both - lax.dot_general(
+                a / pivots,
+                jnp.concatenate([a, v], axis=1),
+                (((0,), (0,)), ((), ())),
+                preferred_element_type=jnp.float32,
+                precision=lax.Precision.HIGHEST,
+            )
+    inverse_factor = jnp.concatenate(solved, axis=0)
+    turned_ref[...] = lax.dot_general(
+        inverse_factor,
+        rotation_ref[...],
+        (((0,), (0,)), ((), ())),
+        preferred_element_type=jnp.float32,
+        precision=lax.Precision.HIGHEST,
+    ).astype(jnp.bfloat16)
+
+
+def cluster_kernel(
+    n_cents, local, all_ref, turned_ref, weight_ref, seed_ref, offset_ref, energy_ref, center_ref,
+    pick, scores, probs, across, mine, theirs, send_sem, recv_sem,
+):
+    group, row = lax.axis_index("groups"), lax.axis_index("rows")
+    me = lax.axis_index("cents")
+    total_rows, width = all_ref.shape
+    count = center_ref.shape[0]
+    chunk = 128
+
+    def peer(step):
+        return (group, row, lax.rem(me + step, n_cents))
+
+    barrier = pltpu.get_barrier_semaphore()
+    for step in range(1, n_cents):
+        pl.semaphore_signal(barrier, inc=1, device_id=peer(step), device_id_type=MESH)
+
+    for at in range(0, total_rows, chunk):
+        ids = lax.broadcasted_iota(jnp.int32, (chunk, count), 0) + at
+        pick[at : at + chunk, :] = jnp.where(ids == seed_ref[...], 1.0, 0.0).astype(jnp.bfloat16)
+
+    mixed = jnp.dot(all_ref[...], turned_ref[...], preferred_element_type=jnp.float32)
+    length = jnp.sum(mixed * mixed, axis=1, keepdims=True)
+    unit = (mixed * lax.rsqrt(length + 1e-06)).astype(jnp.bfloat16)
+    turned_unit = unit.astype(jnp.float32).T
+    norm = jnp.sum(turned_unit * turned_unit, axis=0, keepdims=True)
+    across[...] = turned_unit.astype(jnp.bfloat16)
+    picked = jnp.dot(across[...], pick[...], preferred_element_type=jnp.float32)
+    center_ref[...] = picked.T + offset_ref[...]
+    pl.semaphore_wait(barrier, n_cents - 1)
+
+    scale = LOG2E / sharpness_scale
+    for turn in range(ITERS):
+        peak8 = jnp.full((8, total_rows), -jnp.inf, jnp.float32)
+        for at in range(0, count, chunk):
+            center = center_ref[at : at + chunk, :]
+            square = jnp.sum(center * center, axis=1, keepdims=True) * scale
+            dots = jnp.dot(center.astype(jnp.bfloat16), across[...], preferred_element_type=jnp.float32)
+            score = dots * (2.0 * scale) - square
+            scores[at : at + chunk, :] = score
+            peak8 = jnp.maximum(peak8, jnp.max(score.reshape(chunk // 8, 8, total_rows), axis=0))
+        peak = jnp.max(peak8, axis=0, keepdims=True)
+        total8 = jnp.zeros((8, total_rows), jnp.float32)
+        for at in range(0, count, chunk):
+            prob = jnp.exp2(scores[at : at + chunk, :] - peak)
+            probs[at : at + chunk, :] = prob.astype(jnp.bfloat16)
+            total8 = total8 + jnp.sum(prob.reshape(chunk // 8, 8, total_rows), axis=0)
+        total = jnp.sum(total8, axis=0, keepdims=True)
+        mine[turn, 0:1, :] = peak
+        mine[turn, 1:2, :] = total
+        copies = []
+        for step in range(1, n_cents):
+            copy = pltpu.make_async_remote_copy(
+                src_ref=mine.at[turn],
+                dst_ref=theirs.at[turn, step - 1],
+                send_sem=send_sem.at[turn, step - 1],
+                recv_sem=recv_sem.at[turn, step - 1],
+                device_id=peer(step),
+                device_id_type=MESH,
+            )
+            copy.start()
+            copies.append(copy)
+        for copy in copies:
+            copy.wait()
+        top = peak
+        for step in range(1, n_cents):
+            top = jnp.maximum(top, theirs[turn, step - 1, 0:1, :])
+        own = jnp.exp2(peak - top)
+        whole = total * own
+        for step in range(1, n_cents):
+            whole = whole + theirs[turn, step - 1, 1:2, :] * jnp.exp2(theirs[turn, step - 1, 0:1, :] - top)
+        share = weight_ref[...] * own / whole
+        high = share.astype(jnp.bfloat16).astype(jnp.float32)
+        sub = lax.broadcasted_iota(jnp.int32, (16, total_rows), 0)
+        tail = jnp.where(sub == 0, high, jnp.where(sub == 1, share - high, 0.0)).astype(jnp.bfloat16)
+        moved = jnp.concatenate(
+            [
+                (across[...].astype(jnp.float32) * share).astype(jnp.bfloat16),
+                tail,
+                jnp.zeros((width - 16, total_rows), jnp.bfloat16),
+            ],
+            axis=0,
+        )
+        for at in range(0, count, 256):
+            sums = lax.dot_general(
+                probs[at : at + 256, :], moved, (((1,), (1,)), ((), ())), preferred_element_type=jnp.float32
+            )
+            mass = sums[:, width : width + 1] + sums[:, width + 1 : width + 2]
+            center_ref[at : at + 256, :] = (sums[:, :width] + center_ref[at : at + 256, :]) / (mass + 1.0)
+        if turn == ITERS - 1:
+            energy = top * LN2 + jnp.log(whole) - norm / sharpness_scale
+            index = row * n_cents + me
+            kept = jnp.zeros((1, local), jnp.float32)
+            for place in range(total_rows // local):
+                kept = jnp.where(index == place, energy[:, place * local : (place + 1) * local], kept)
+            energy_ref[...] = kept
+
+
+def gathered_shards(n_rows, n_cents, embedding, degrees, rotation, offsets, seed_ids):
+    local, width = embedding.shape
+    members = n_rows * n_cents
+    total_rows = local * members
+    count = offsets.shape[0]
+    everyone, weight, shifted = pl.pallas_call(
+        functools.partial(gather_kernel, n_rows, n_cents),
+        out_shape=(
+            jax.ShapeDtypeStruct((total_rows, width), jnp.bfloat16),
+            jax.ShapeDtypeStruct((1, total_rows), jnp.float32),
+            jax.ShapeDtypeStruct((width, width), jnp.float32),
+        ),
+        in_specs=vmem(2),
+        out_specs=tuple(vmem(3)),
+        scratch_shapes=[
+            pltpu.VMEM((members, local + 16, width), jnp.bfloat16),
+            pltpu.SemaphoreType.DMA((members - 1,)),
+            pltpu.SemaphoreType.DMA((members - 1,)),
+        ],
+        compiler_params=pltpu.CompilerParams(collective_id=0, has_side_effects=True),
+    )(embedding, degrees.reshape(1, local))
+    turned = pl.pallas_call(
+        factor_kernel,
+        out_shape=jax.ShapeDtypeStruct((width, width), jnp.bfloat16),
+        in_specs=vmem(2),
+        out_specs=vmem(1)[0],
+    )(shifted, rotation)
+    energy, centers = pl.pallas_call(
+        functools.partial(cluster_kernel, n_cents, local),
+        out_shape=(
+            jax.ShapeDtypeStruct((1, local), jnp.float32),
+            jax.ShapeDtypeStruct((count, width), jnp.float32),
+        ),
+        in_specs=vmem(5),
+        out_specs=tuple(vmem(2)),
+        scratch_shapes=[
+            pltpu.VMEM((total_rows, count), jnp.bfloat16),
+            pltpu.VMEM((count, total_rows), jnp.float32),
+            pltpu.VMEM((count, total_rows), jnp.bfloat16),
+            pltpu.VMEM((width, total_rows), jnp.bfloat16),
+            pltpu.VMEM((ITERS, 2, total_rows), jnp.float32),
+            pltpu.VMEM((ITERS, n_cents - 1, 2, total_rows), jnp.float32),
+            pltpu.SemaphoreType.DMA((ITERS, n_cents - 1)),
+            pltpu.SemaphoreType.DMA((ITERS, n_cents - 1)),
+        ],
+        compiler_params=pltpu.CompilerParams(
+            collective_id=1, has_side_effects=True, vmem_limit_bytes=40 * 1024 * 1024
+        ),
+    )(everyone, turned, weight, seed_ids.reshape(1, count), offsets)
+    return energy.reshape(local), centers
+
+
 def solution(mesh):
+    n_rows, n_cents = mesh.shape["rows"], mesh.shape["cents"]
+
+    def program(embedding, degrees, rotation, offsets, seed_ids):
+        if embedding.shape[0] * n_rows * n_cents <= GATHER_ROWS:
+            return gathered_shards(n_rows, n_cents, embedding, degrees, rotation, offsets, seed_ids)
+        return shards(embedding, degrees, rotation, offsets, seed_ids)
+
     placed = (
         P(("groups", "rows", "cents"), None),
         P(("groups", "rows", "cents")),
@@ -140,7 +400,7 @@
         P(("groups", "cents")),
     )
     return jax.shard_map(
-        shards,
+        program,
         mesh=mesh,
         in_specs=placed,
         out_specs=(P(("groups", "rows", "cents")), P(("groups", "cents"), None)),

time: 815 us -> 46.2 us (0.06)
  local copies, waits for them, and re-layouts: 225 us -> 4.06 us
  matrix products: 218 us -> 0 us
  waiting for transfers between devices: 167 us -> 0 us
  loops' own time: 96.5 us -> 0 us
  blocking collectives: 79.4 us -> 0 us
  Pallas kernels: 0 us -> 41.1 us
  between operations: 14.6 us -> 0.67 us
  other arithmetic: 8.24 us -> 0 us
    dot_general x263 -> x0, matrix products: 218 us -> none  [the longest x128 190 us: row_step(): jnp.dot(column, solved, precision=lax.Precision.HIGHEST)]
    psum x4 -> x0, waiting for transfers between devices: 167 us -> none  [the longest x1 73.5 us: shards(): gram = lax.psum(partial_gram_matrix, ('rows', 'cents'))]
    dynamic_slice x256 -> x0, local copies, waits for them, and re-layouts: 157 us -> none  [the longest x128 81.4 us: column_step(): pivot = jnp.sqrt(lax.dynamic_index_in_dim(column, index, 0, keepdims=False))]
    another operation x2 -> x0, loops' own time: 96.5 us -> none  [the longest x1 92.7 us: lower_factor(): lax.fori_loop(0, width, column_step, jnp.zeros(matrix.shape, matrix.dtype))]
    dynamic_update_slice x256 -> x0, local copies, waits for them, and re-layouts: 49.8 us -> none  [the longest x128 45.9 us: column_step(): return lax.dynamic_update_slice_in_dim(factor, column[:, None], index, 1)]
    pallas_call x0 -> x3, Pallas kernels: none -> 41.1 us  [the longest x1 16.1 us: gathered_shards(): pl.pallas_call(functools.partial(gather_kernel, n_rows, n_cents), out_sha...]
    psum x4 -> x0, blocking collectives: 28.4 us -> none  [the longest x2 16.7 us: shards(): whole = lax.psum(totals * jnp.exp(peaks - larger), 'cents')]
    pmax x2 -> x0, blocking collectives: 23.4 us -> none  [shards(): larger = lax.pmax(peaks, 'cents')]
  transfers between devices with their start and end apart: 4 -> 0, of which waited for: 4 -> 0; matrix products, arithmetic and copies ran while one was open for 0% -> 0% of each run, Pallas kernels for 0% -> 0%
where the time goes in v1:
time: 46.2 us; the launch traced here: 45.8 us
  Pallas kernels  41.1 us (89%)
  local copies, waits for them, and re-layouts  4.06 us (9%)
  between operations  0.67 us (1%)
    pallas_call x1, Pallas kernels, gathered_shards(): pl.pallas_call(functools.partial(gather_kernel, n_rows, n_cents), out_sha...  16.1 us
    pallas_call x1, Pallas kernels, gathered_shards(): pl.pallas_call(functools.partial(cluster_kernel, n_cents, local), out_sha...  14.8 us
    pallas_call x1, Pallas kernels, gathered_shards(): pl.pallas_call(factor_kernel, out_shape=jax.ShapeDtypeStruct((width, widt...  10.2 us
    unnamed x12, local copies, waits for them, and re-layouts  4.06 us

profile of v1, /device:TPU:0, one launch (start us, length us, event | category | flops | bytes accessed | tf_op | source)
XLA Modules:
  0.0 45.8 jit_solution(11053664358383307518)
XLA Ops:
  0.6 16.1 %shard_map.68 = (bf16[1024,128]{1,0:T(8,128)(2,1)}, f32[1,1024]{1,0:T(1,128)}, f32[128,128]{1,0:T(8,128)}) custom-call(bf16[64,128]{1,0:T(8,128)(2,1)} %emb_ref.1, s32[1,64]{1,0:T(1,128)} %bitcast.5), custom_call_target="tpu_custom_call" | custom-call | tf_op jit(solution)/shard_map/pallas_call | solution.py:340
  16.8 0.0 copy-start.3
  16.8 0.0 copy-start.4
  16.8 10.2 %shard_map.69.turned_ref = bf16[128,128]{1,0:T(8,128)(2,1)} custom-call(f32[128,128]{1,0:T(8,128)} %get-tuple-element.8.matrix_ref, f32[128,128]{1,0:T(8,128)} %rotation_ref.1), custom_call_target="tpu_custom_call" | custom-call | tf_op jit(solution)/shard_map/pallas_call | solution.py:356
  27.0 0.0 copy-done.3
  27.0 0.0 copy-done.4
  27.0 0.0 copy-start
  27.0 1.0 %copy-done = f32[1024,128]{1,0:T(8,128)S(1)} copy-done((f32[1024,128]{1,0:T(8,128)S(1)}, f32[1024,128]{1,0:T(8,128)}, u32[]{:S(2)}) %copy-start) | copy-done | bytes 524312
  28.0 0.0 copy-start.1
  28.0 0.9 %copy-done.1 = bf16[1024,128]{1,0:T(8,128)(2,1)S(1)} copy-done((bf16[1024,128]{1,0:T(8,128)(2,1)S(1)}, bf16[1024,128]{1,0:T(8,128)(2,1)}, u32[]{:S(2)}) %copy-start.1) | copy-done | bytes 262168
  29.0 0.0 copy-start.2
  29.0 0.8 %copy-done.2 = bf16[128,128]{1,0:T(8,128)(2,1)S(1)} copy-done((bf16[128,128]{1,0:T(8,128)(2,1)S(1)}, bf16[128,128]{1,0:T(8,128)(2,1)}, u32[]{:S(2)}) %copy-start.2) | copy-done | bytes 32792
  29.7 14.8 %shard_map.70 = (f32[1,64]{1,0:T(1,128)S(1)}, f32[1024,128]{1,0:T(8,128)S(1)}) custom-call(bf16[1024,128]{1,0:T(8,128)(2,1)S(1)} %copy-done.1, bf16[128,128]{1,0:T(8,128)(2,1)S(1)} %copy-done.2, f32[1,1024]{1,0:T(1,128)S(1)} %copy-done.4, s32[1,1024]{1,0:T(1,128)S(1)} %bitcast.3, f32[1024,128]{1,0:T(8,128)S(1)} %copy-done), custom_call_target="tpu_custom_call" | custom-call | tf_op jit(solution)/shard_map/pallas_call | solution.py:362
  44.5 0.5 %copy.9 = f32[64]{0:T(128)} copy(f32[64]{0:T(128)S(1)} %bitcast.4) | data formatting | bytes 512
  45.0 0.8 %copy.10 = f32[1024,128]{1,0:T(8,128)} copy(f32[1024,128]{1,0:T(8,128)S(1)} %get-tuple-element.15) | data formatting | bytes 1048576
Async XLA Ops:
  16.8 10.2 %copy-start.3 = (s32[1024]{0:T(1024)S(1)}, s32[1024]{0:T(1024)}, u32[]{:S(2)}) copy-start(s32[1024]{0:T(1024)} %param.9) | copy-start | bytes 12292
  16.8 10.2 %copy-start.4 = (f32[1,1024]{1,0:T(1,128)S(1)}, f32[1,1024]{1,0:T(1,128)}, u32[]{:S(2)}) copy-start(f32[1,1024]{1,0:T(1,128)} %get-tuple-element.9.weight_ref) | copy-start | bytes 12292
  27.0 1.0 %copy-start = (f32[1024,128]{1,0:T(8,128)S(1)}, f32[1024,128]{1,0:T(8,128)}, u32[]{:S(2)}) copy-start(f32[1024,128]{1,0:T(8,128)} %offset_ref.1) | copy-start | bytes 1572868
  28.0 0.9 %copy-start.1 = (bf16[1024,128]{1,0:T(8,128)(2,1)S(1)}, bf16[1024,128]{1,0:T(8,128)(2,1)}, u32[]{:S(2)}) copy-start(bf16[1024,128]{1,0:T(8,128)(2,1)} %get-tuple-element.7.all_ref) | copy-start | bytes 786436
  29.0 0.8 %copy-start.2 = (bf16[128,128]{1,0:T(8,128)(2,1)S(1)}, bf16[128,128]{1,0:T(8,128)(2,1)}, u32[]{:S(2)}) copy-start(bf16[128,128]{1,0:T(8,128)(2,1)} %shard_map.69.turned_ref) | copy-start | bytes 98308

commit v2 on v1

--- a/solution.py
+++ b/solution.py
@@ -139,131 +139,179 @@
 MESH = pl.DeviceIdType.MESH
 LOG2E = math.log2(math.e)
 LN2 = math.log(2.0)
-GATHER_ROWS = 2048
-BLOCK = 8
-
-
-def vmem(count):
-    return [pl.BlockSpec(memory_space=pltpu.VMEM)] * count
-
-
-def gather_kernel(n_rows, n_cents, emb_ref, deg_ref, all_ref, weight_ref, shifted_ref, held, send_sem, recv_sem):
-    group = lax.axis_index("groups")
-    me = lax.axis_index("rows") * n_cents + lax.axis_index("cents")
-    members = n_rows * n_cents
-    local, width = emb_ref.shape
-
-    def peer(step):
-        other = lax.rem(me + step, members)
-        return (group, other // n_cents, lax.rem(other, n_cents))
-
-    barrier = pltpu.get_barrier_semaphore()
-    for step in range(1, members):
-        pl.semaphore_signal(barrier, inc=1, device_id=peer(step), device_id_type=MESH)
-    held[me, :local, :] = emb_ref[...]
-    tag = jnp.concatenate(
-        [deg_ref[...].astype(jnp.float32), jnp.zeros((1, width - local), jnp.float32)], axis=1
-    )
-    held[me, local:, :] = jnp.broadcast_to(tag, (16, width)).astype(jnp.bfloat16)
-    pl.semaphore_wait(barrier, members - 1)
-    copies = []
-    for step in range(1, members):
-        copy = pltpu.make_async_remote_copy(
-            src_ref=held.at[me],
-            dst_ref=held.at[me],
-            send_sem=send_sem.at[step - 1],
-            recv_sem=recv_sem.at[step - 1],
-            device_id=peer(step),
-            device_id_type=MESH,
-        )
-        copy.start()
-        copies.append(copy)
-    for copy in copies:
-        copy.wait()
-    rows = held[:, :local, :].reshape(members * local, width)
-    all_ref[...] = rows
-    gram = lax.dot_general(rows, rows, (((0,), (0,)), ((), ())), preferred_element_type=jnp.float32)
-    eye = lax.broadcasted_iota(jnp.int32, gram.shape, 0) == lax.broadcasted_iota(jnp.int32, gram.shape, 1)
-    shifted_ref[...] = gram / (members * local) + jnp.where(eye, ridge, 0.0)
-    tags = held[:, local:, :].astype(jnp.float32)
-    weight_ref[...] = jnp.sqrt(
-        jnp.concatenate([tags[index, :1, :local] for index in range(members)], axis=1)
-    )
-
-
-def factor_kernel(matrix_ref, rotation_ref, turned_ref):
-    width = matrix_ref.shape[0]
-    left = matrix_ref[...]
+VMEM_LIMIT = 56 * 1024 * 1024
+BLOCK = 32
+
+
+def inverse_factor(matrix):
+    width = matrix.shape[0]
     row_id = lax.broadcasted_iota(jnp.int32, (width, width), 0)
     col_id = lax.broadcasted_iota(jnp.int32, (width, width), 1)
+    left = matrix
     right = jnp.where(row_id == col_id, 1.0, 0.0).astype(jnp.float32)
-    both = jnp.concatenate([left, right], axis=1)
     sub = lax.broadcasted_iota(jnp.int32, (BLOCK, width), 0)
     solved = []
-    for block in range(width // BLOCK):
-        at = block * BLOCK
-        a = both[at : at + BLOCK, :width]
-        v = both[at : at + BLOCK, width:]
+    for at in range(0, width, BLOCK):
+        a, v = left[:BLOCK], right[:BLOCK]
         columns = [jnp.broadcast_to(a[:, at + j : at + j + 1], (BLOCK, width)) for j in range(BLOCK)]
         pivots = jnp.ones((BLOCK, width), jnp.float32)
         for j in range(BLOCK):
+            low = j // 8 * 8
+
+            def lower(old, new):
+                return new if low == 0 else jnp.concatenate([old[:low], new], axis=0)
+
             pivot = columns[j][j : j + 1, :]
-            inverse = 1.0 / pivot
             pivots = jnp.where(sub == j, pivot, pivots)
-            share = jnp.where(sub > j, columns[j] * inverse, 0.0)
+            share = jnp.where(sub[low:] > j, columns[j][low:] * (1.0 / pivot), 0.0)
             for l in range(j + 1, BLOCK):
-                columns[l] = columns[l] - share * columns[l][j : j + 1, :]
-            a = a - share * a[j : j + 1, :]
-            v = v - share * v[j : j + 1, :]
+                columns[l] = lower(columns[l], columns[l][low:] - share * columns[l][j : j + 1, :])
+            a = lower(a, a[low:] - share * a[j : j + 1, :])
+            v = lower(v, v[low:] - share * v[j : j + 1, :])
         solved.append(v * lax.rsqrt(pivots))
         if at + BLOCK < width:
-            both = both - lax.dot_general(
+            update = lax.dot_general(
                 a / pivots,
                 jnp.concatenate([a, v], axis=1),
                 (((0,), (0,)), ((), ())),
                 preferred_element_type=jnp.float32,
                 precision=lax.Precision.HIGHEST,
-            )
-    inverse_factor = jnp.concatenate(solved, axis=0)
-    turned_ref[...] = lax.dot_general(
-        inverse_factor,
-        rotation_ref[...],
+            )[at + BLOCK :]
+            left = left[BLOCK:] - update[:, :width]
+            right = right[BLOCK:] - update[:, width:]
+    return jnp.concatenate(solved, axis=0)
+
+
+def embed_kernel(
+    n_rows, n_cents, emb_hbm, deg_hbm, rotation_hbm, offset_hbm, seed_hbm, energy_ref, center_ref,
+    held, degree, rotation, offset, seeds, pick, scores, probs, across, mine, theirs,
+    load_sem, near_send, near_recv, side_send, side_recv, mate_send, mate_recv, send_sem, recv_sem,
+):
+    group, row, me = lax.axis_index("groups"), lax.axis_index("rows"), lax.axis_index("cents")
+    local, width = emb_hbm.shape
+    members = n_rows * n_cents
+    total_rows = members * local
+    count = center_ref.shape[0]
+    half = n_rows // 2
+    chunk = 128
+
+    loads = [
+        pltpu.make_async_copy(source, target, load_sem.at[index])
+        for index, (source, target) in enumerate(
+            (
+                (emb_hbm, held.at[row * n_cents + me, pl.ds(0, local)]),
+                (deg_hbm, degree),
+                (seed_hbm, seeds),
+                (rotation_hbm, rotation),
+                (offset_hbm, offset),
+            )
+        )
+    ]
+    for load in loads:
+        load.start()
+
+    def cent(step):
+        return lax.rem(me + step + n_cents, n_cents)
+
+    def side(step):
+        return lax.rem(row + 2 * step + n_rows, n_rows)
+
+    mate = row + 1 - 2 * lax.rem(row, 2)
+    barrier = pltpu.get_barrier_semaphore()
+    peers = [(group, row, cent(step)) for step in range(1, n_cents)]
+    peers += [(group, side(step), me) for step in range(1, half)] + [(group, mate, me)]
+    for device in peers:
+        pl.semaphore_signal(barrier, inc=1, device_id=device, device_id_type=MESH)
+
+    def fill(first, last):
+        for at in range(first, last, chunk):
+            ids = lax.broadcasted_iota(jnp.int32, (chunk, count), 0) + at
+            pick[at : at + chunk, :] = jnp.where(ids == seeds[...], 1.0, 0.0).astype(jnp.bfloat16)
+
+    def pushed(slot, send, recv, device):
+        return pltpu.make_async_remote_copy(
+            src_ref=held.at[slot],
+            dst_ref=held.at[slot],
+            send_sem=send,
+            recv_sem=recv,
+            device_id=device,
+            device_id_type=MESH,
+        )
+
+    loads[1].wait()
+    tag = jnp.concatenate(
+        [degree[...].astype(jnp.float32), jnp.zeros((1, width - local), jnp.float32)], axis=1
+    )
+    held[row * n_cents + me, local:, :] = jnp.broadcast_to(tag, (16, width)).astype(jnp.bfloat16)
+    loads[0].wait()
+    pl.semaphore_wait(barrier, len(peers))
+    near = [
+        pushed(row * n_cents + me, near_send.at[step - 1], near_recv.at[step - 1], (group, row, cent(step)))
+        for step in range(1, n_cents)
+    ]
+    for copy in near:
+        copy.start()
+    sides, mates = [], []
+
+    def to_side(step):
+        for other in range(1, half):
+            place = (other - 1) * n_cents + step
+            copy = pushed(
+                row * n_cents + cent(-step), side_send.at[place], side_recv.at[place], (group, side(other), me)
+            )
+            copy.start()
+            sides.append(copy)
+
+    def to_mate(other, step):
+        place = other * n_cents + step
+        copy = pushed(
+            side(-other) * n_cents + cent(-step), mate_send.at[place], mate_recv.at[place], (group, mate, me)
+        )
+        copy.start()
+        mates.append(copy)
+
+    to_side(0)
+    to_mate(0, 0)
+    loads[2].wait()
+    fill(0, total_rows // 2)
+    for step in range(1, n_cents):
+        near[step - 1].wait_recv()
+        to_side(step)
+        to_mate(0, step)
+    fill(total_rows // 2, total_rows)
+    for step in range(n_cents):
+        for other in range(1, half):
+            sides[step * (half - 1) + other - 1].wait_recv()
+            to_mate(other, step)
+    for copy in mates:
+        copy.wait_recv()
+    for copy in near + sides + mates:
+        copy.wait_send()
+
+    rows = held[:, :local, :].reshape(total_rows, width)
+    gram = lax.dot_general(rows, rows, (((0,), (0,)), ((), ())), preferred_element_type=jnp.float32)
+    eye = lax.broadcasted_iota(jnp.int32, gram.shape, 0) == lax.broadcasted_iota(jnp.int32, gram.shape, 1)
+    shifted = gram / total_rows + jnp.where(eye, ridge, 0.0)
+    tags = held[:, local:, :].astype(jnp.float32)
+    weight = jnp.sqrt(jnp.concatenate([tags[index, :1, :local] for index in range(members)], axis=1))
+    loads[3].wait()
+    turned = lax.dot_general(
+        inverse_factor(shifted),
+        rotation[...],
         (((0,), (0,)), ((), ())),
         preferred_element_type=jnp.float32,
         precision=lax.Precision.HIGHEST,
     ).astype(jnp.bfloat16)
 
-
-def cluster_kernel(
-    n_cents, local, all_ref, turned_ref, weight_ref, seed_ref, offset_ref, energy_ref, center_ref,
-    pick, scores, probs, across, mine, theirs, send_sem, recv_sem,
-):
-    group, row = lax.axis_index("groups"), lax.axis_index("rows")
-    me = lax.axis_index("cents")
-    total_rows, width = all_ref.shape
-    count = center_ref.shape[0]
-    chunk = 128
-
-    def peer(step):
-        return (group, row, lax.rem(me + step, n_cents))
-
-    barrier = pltpu.get_barrier_semaphore()
-    for step in range(1, n_cents):
-        pl.semaphore_signal(barrier, inc=1, device_id=peer(step), device_id_type=MESH)
-
-    for at in range(0, total_rows, chunk):
-        ids = lax.broadcasted_iota(jnp.int32, (chunk, count), 0) + at
-        pick[at : at + chunk, :] = jnp.where(ids == seed_ref[...], 1.0, 0.0).astype(jnp.bfloat16)
-
-    mixed = jnp.dot(all_ref[...], turned_ref[...], preferred_element_type=jnp.float32)
+    mixed = jnp.dot(rows, turned, preferred_element_type=jnp.float32)
     length = jnp.sum(mixed * mixed, axis=1, keepdims=True)
     unit = (mixed * lax.rsqrt(length + 1e-06)).astype(jnp.bfloat16)
     turned_unit = unit.astype(jnp.float32).T
     norm = jnp.sum(turned_unit * turned_unit, axis=0, keepdims=True)
     across[...] = turned_unit.astype(jnp.bfloat16)
     picked = jnp.dot(across[...], pick[...], preferred_element_type=jnp.float32)
-    center_ref[...] = picked.T + offset_ref[...]
-    pl.semaphore_wait(barrier, n_cents - 1)
+    loads[4].wait()
+    center_ref[...] = picked.T + offset[...]
 
     scale = LOG2E / sharpness_scale
     for turn in range(ITERS):
@@ -291,7 +339,7 @@
                 dst_ref=theirs.at[turn, step - 1],
                 send_sem=send_sem.at[turn, step - 1],
                 recv_sem=recv_sem.at[turn, step - 1],
-                device_id=peer(step),
+                device_id=(group, row, cent(step)),
                 device_id_type=MESH,
             )
             copy.start()
@@ -305,7 +353,7 @@
         whole = total * own
         for step in range(1, n_cents):
             whole = whole + theirs[turn, step - 1, 1:2, :] * jnp.exp2(theirs[turn, step - 1, 0:1, :] - top)
-        share = weight_ref[...] * own / whole
+        share = weight * own / whole
         high = share.astype(jnp.bfloat16).astype(jnp.float32)
         sub = lax.broadcasted_iota(jnp.int32, (16, total_rows), 0)
         tail = jnp.where(sub == 0, high, jnp.where(sub == 1, share - high, 0.0)).astype(jnp.bfloat16)
@@ -327,9 +375,23 @@
             energy = top * LN2 + jnp.log(whole) - norm / sharpness_scale
             index = row * n_cents + me
             kept = jnp.zeros((1, local), jnp.float32)
-            for place in range(total_rows // local):
+            for place in range(members):
                 kept = jnp.where(index == place, energy[:, place * local : (place + 1) * local], kept)
             energy_ref[...] = kept
+
+
+def fits(n_rows, n_cents, local, width, count):
+    total_rows = n_rows * n_cents * local
+    return (
+        n_rows % 2 == 0
+        and n_cents > 1
+        and width == 128
+        and local <= width
+        and local % 16 == 0
+        and count % 256 == 0
+        and total_rows % 256 == 0
+        and total_rows * count <= 2 * 1024 * 1024
+    )
 
 
 def gathered_shards(n_rows, n_cents, embedding, degrees, rotation, offsets, seed_ids):
@@ -337,50 +399,43 @@
     members = n_rows * n_cents
     total_rows = local * members
     count = offsets.shape[0]
-    everyone, weight, shifted = pl.pallas_call(
-        functools.partial(gather_kernel, n_rows, n_cents),
-        out_shape=(
-            jax.ShapeDtypeStruct((total_rows, width), jnp.bfloat16),
-            jax.ShapeDtypeStruct((1, total_rows), jnp.float32),
-            jax.ShapeDtypeStruct((width, width), jnp.float32),
-        ),
-        in_specs=vmem(2),
-        out_specs=tuple(vmem(3)),
-        scratch_shapes=[
-            pltpu.VMEM((members, local + 16, width), jnp.bfloat16),
-            pltpu.SemaphoreType.DMA((members - 1,)),
-            pltpu.SemaphoreType.DMA((members - 1,)),
-        ],
-        compiler_params=pltpu.CompilerParams(collective_id=0, has_side_effects=True),
-    )(embedding, degrees.reshape(1, local))
-    turned = pl.pallas_call(
-        factor_kernel,
-        out_shape=jax.ShapeDtypeStruct((width, width), jnp.bfloat16),
-        in_specs=vmem(2),
-        out_specs=vmem(1)[0],
-    )(shifted, rotation)
+    half = n_rows // 2
+    sides = max(half - 1, 1) * n_cents
+    dma = pltpu.SemaphoreType.DMA
     energy, centers = pl.pallas_call(
-        functools.partial(cluster_kernel, n_cents, local),
+        functools.partial(embed_kernel, n_rows, n_cents),
         out_shape=(
             jax.ShapeDtypeStruct((1, local), jnp.float32),
             jax.ShapeDtypeStruct((count, width), jnp.float32),
         ),
-        in_specs=vmem(5),
-        out_specs=tuple(vmem(2)),
+        in_specs=[pl.BlockSpec(memory_space=pl.ANY)] * 5,
+        out_specs=(pl.BlockSpec(memory_space=pltpu.VMEM),) * 2,
         scratch_shapes=[
+            pltpu.VMEM((members, local + 16, width), jnp.bfloat16),
+            pltpu.VMEM((1, local), jnp.int32),
+            pltpu.VMEM((width, width), jnp.float32),
+            pltpu.VMEM((count, width), jnp.float32),
+            pltpu.VMEM((1, count), jnp.int32),
             pltpu.VMEM((total_rows, count), jnp.bfloat16),
             pltpu.VMEM((count, total_rows), jnp.float32),
             pltpu.VMEM((count, total_rows), jnp.bfloat16),
             pltpu.VMEM((width, total_rows), jnp.bfloat16),
             pltpu.VMEM((ITERS, 2, total_rows), jnp.float32),
             pltpu.VMEM((ITERS, n_cents - 1, 2, total_rows), jnp.float32),
-            pltpu.SemaphoreType.DMA((ITERS, n_cents - 1)),
-            pltpu.SemaphoreType.DMA((ITERS, n_cents - 1)),
+            dma((5,)),
+            dma((n_cents - 1,)),
+            dma((n_cents - 1,)),
+            dma((sides,)),
+            dma((sides,)),
+            dma((half * n_cents,)),
+            dma((half * n_cents,)),
+            dma((ITERS, n_cents - 1)),
+            dma((ITERS, n_cents - 1)),
         ],
         compiler_params=pltpu.CompilerParams(
-            collective_id=1, has_side_effects=True, vmem_limit_bytes=40 * 1024 * 1024
+            collective_id=0, has_side_effects=True, vmem_limit_bytes=VMEM_LIMIT
         ),
-    )(everyone, turned, weight, seed_ids.reshape(1, count), offsets)
+    )(embedding, degrees.reshape(1, local), rotation, offsets, seed_ids.reshape(1, count))
     return energy.reshape(local), centers
 
 
@@ -388,7 +443,7 @@
     n_rows, n_cents = mesh.shape["rows"], mesh.shape["cents"]
 
     def program(embedding, degrees, rotation, offsets, seed_ids):
-        if embedding.shape[0] * n_rows * n_cents <= GATHER_ROWS:
+        if fits(n_rows, n_cents, *embedding.shape, offsets.shape[0]):
             return gathered_shards(n_rows, n_cents, embedding, degrees, rotation, offsets, seed_ids)
         return shards(embedding, degrees, rotation, offsets, seed_ids)
 

time: 46.2 us -> 35.5 us (0.77)
  Pallas kernels: 41.1 us -> 31.6 us
  local copies, waits for them, and re-layouts: 4.06 us -> 3.04 us
    pallas_call x3 -> x1, Pallas kernels: 41.1 us -> 31.6 us  [gathered_shards(): pl.pallas_call(functools.partial(embed_kernel, n_rows, n_cents), out_shap...]
    unnamed x12 -> x4, local copies, waits for them, and re-layouts: 4.06 us -> 3.04 us
where the time goes in v2:
time: 35.5 us; the launch traced here: 35.3 us
  Pallas kernels  31.6 us (89%)
  local copies, waits for them, and re-layouts  3.04 us (9%)
  between operations  0.65 us (2%)
    pallas_call x1, Pallas kernels, gathered_shards(): pl.pallas_call(functools.partial(embed_kernel, n_rows, n_cents), out_shap...  31.6 us
    unnamed x4, local copies, waits for them, and re-layouts  3.04 us

profile of v2, /device:TPU:0, one launch (start us, length us, event | category | flops | bytes accessed | tf_op | source)
XLA Modules:
  0.0 35.3 jit_solution(6586779712419605709)
XLA Ops:
  0.6 31.6 %shard_map.68 = (f32[1,64]{1,0:T(1,128)}, f32[1024,128]{1,0:T(8,128)}) custom-call(bf16[64,128]{1,0:T(8,128)(2,1)} %emb_hbm.1, s32[1,64]{1,0:T(1,128)} %bitcast.4, f32[128,128]{1,0:T(8,128)} %rotation_hbm.1, f32[1024,128]{1,0:T(8,128)} %offset_hbm.1, s32[1,1024]{1,0:T(1,128)} %bitcast.3), custom_call_target="tpu_custom_call" | custom-call | tf_op jit(solution)/shard_map/pallas_call | solution.py:405
  32.2 0.0 copy-start
  32.2 0.7 %copy-done = f32[1,64]{1,0:T(1,128)S(1)} copy-done((f32[1,64]{1,0:T(1,128)S(1)}, f32[1,64]{1,0:T(1,128)}, u32[]{:S(2)}) %copy-start) | copy-done | bytes 280
  32.9 0.5 %copy.9 = f32[64]{0:T(128)} copy(f32[64]{0:T(128)S(1)} %bitcast.5) | data formatting | bytes 512
  33.4 1.9 %copy.10 = f32[1024,128]{1,0:T(8,128)} copy(f32[1024,128]{1,0:T(8,128)} %get-tuple-element.9) | data formatting | bytes 1048576
Async XLA Ops:
  32.2 0.7 %copy-start = (f32[1,64]{1,0:T(1,128)S(1)}, f32[1,64]{1,0:T(1,128)}, u32[]{:S(2)}) copy-start(f32[1,64]{1,0:T(1,128)} %get-tuple-element.4) | copy-start | bytes 772

commit v3 on v2

--- a/solution.py
+++ b/solution.py
@@ -185,7 +185,7 @@
 def embed_kernel(
     n_rows, n_cents, emb_hbm, deg_hbm, rotation_hbm, offset_hbm, seed_hbm, energy_ref, center_ref,
     held, degree, rotation, offset, seeds, pick, scores, probs, across, mine, theirs,
-    load_sem, near_send, near_recv, side_send, side_recv, mate_send, mate_recv, send_sem, recv_sem,
+    load_sem, near_send, near_recv, mate_send, mate_recv, send_sem, recv_sem,
 ):
     group, row, me = lax.axis_index("groups"), lax.axis_index("rows"), lax.axis_index("cents")
     local, width = emb_hbm.shape
@@ -218,8 +218,8 @@
 
     mate = row + 1 - 2 * lax.rem(row, 2)
     barrier = pltpu.get_barrier_semaphore()
-    peers = [(group, row, cent(step)) for step in range(1, n_cents)]
-    peers += [(group, side(step), me) for step in range(1, half)] + [(group, mate, me)]
+    far = [(other, step) for step in range(n_cents) for other in range(half)][1:]
+    peers = [(group, side(other), cent(step)) for other, step in far] + [(group, mate, me)]
     for device in peers:
         pl.semaphore_signal(barrier, inc=1, device_id=device, device_id_type=MESH)
 
@@ -244,48 +244,27 @@
     )
     held[row * n_cents + me, local:, :] = jnp.broadcast_to(tag, (16, width)).astype(jnp.bfloat16)
     loads[0].wait()
+    loads[2].wait()
+    fill(0, total_rows)
     pl.semaphore_wait(barrier, len(peers))
-    near = [
-        pushed(row * n_cents + me, near_send.at[step - 1], near_recv.at[step - 1], (group, row, cent(step)))
-        for step in range(1, n_cents)
-    ]
-    for copy in near:
+    near, mates = [], []
+    for place, (other, step) in enumerate(far):
+        copy = pushed(
+            row * n_cents + me, near_send.at[place], near_recv.at[place], (group, side(other), cent(step))
+        )
         copy.start()
-    sides, mates = [], []
-
-    def to_side(step):
-        for other in range(1, half):
-            place = (other - 1) * n_cents + step
-            copy = pushed(
-                row * n_cents + cent(-step), side_send.at[place], side_recv.at[place], (group, side(other), me)
-            )
-            copy.start()
-            sides.append(copy)
-
-    def to_mate(other, step):
-        place = other * n_cents + step
+        near.append(copy)
+    for place, (other, step) in enumerate([(0, 0)] + far):
+        if place:
+            near[place - 1].wait_recv()
         copy = pushed(
             side(-other) * n_cents + cent(-step), mate_send.at[place], mate_recv.at[place], (group, mate, me)
         )
         copy.start()
         mates.append(copy)
-
-    to_side(0)
-    to_mate(0, 0)
-    loads[2].wait()
-    fill(0, total_rows // 2)
-    for step in range(1, n_cents):
-        near[step - 1].wait_recv()
-        to_side(step)
-        to_mate(0, step)
-    fill(total_rows // 2, total_rows)
-    for step in range(n_cents):
-        for other in range(1, half):
-            sides[step * (half - 1) + other - 1].wait_recv()
-            to_mate(other, step)
     for copy in mates:
         copy.wait_recv()
-    for copy in near + sides + mates:
+    for copy in near + mates:
         copy.wait_send()
 
     rows = held[:, :local, :].reshape(total_rows, width)
@@ -380,6 +359,11 @@
             energy_ref[...] = kept
 
 
+def finish_kernel(energy_in, center_in, energy_out, center_out):
+    energy_out[...] = energy_in[...]
+    center_out[...] = center_in[...]
+
+
 def fits(n_rows, n_cents, local, width, count):
     total_rows = n_rows * n_cents * local
     return (
@@ -400,7 +384,6 @@
     total_rows = local * members
     count = offsets.shape[0]
     half = n_rows // 2
-    sides = max(half - 1, 1) * n_cents
     dma = pltpu.SemaphoreType.DMA
     energy, centers = pl.pallas_call(
         functools.partial(embed_kernel, n_rows, n_cents),
@@ -423,10 +406,8 @@
             pltpu.VMEM((ITERS, 2, total_rows), jnp.float32),
             pltpu.VMEM((ITERS, n_cents - 1, 2, total_rows), jnp.float32),
             dma((5,)),
-            dma((n_cents - 1,)),
-            dma((n_cents - 1,)),
-            dma((sides,)),
-            dma((sides,)),
+            dma((half * n_cents - 1,)),
+            dma((half * n_cents - 1,)),
             dma((half * n_cents,)),
             dma((half * n_cents,)),
             dma((ITERS, n_cents - 1)),
@@ -436,6 +417,15 @@
             collective_id=0, has_side_effects=True, vmem_limit_bytes=VMEM_LIMIT
         ),
     )(embedding, degrees.reshape(1, local), rotation, offsets, seed_ids.reshape(1, count))
+    energy, centers = pl.pallas_call(
+        finish_kernel,
+        out_shape=(
+            jax.ShapeDtypeStruct((1, local), jnp.float32),
+            jax.ShapeDtypeStruct((count, width), jnp.float32),
+        ),
+        in_specs=[pl.BlockSpec(memory_space=pltpu.VMEM)] * 2,
+        out_specs=(pl.BlockSpec(memory_space=pltpu.VMEM),) * 2,
+    )(energy, centers)
     return energy.reshape(local), centers
 
 

time: 35.5 us -> 33 us (0.930)
  local copies, waits for them, and re-layouts: 3.04 us -> 0 us
  Pallas kernels: 31.6 us -> 32.1 us
    unnamed x4 -> x0, local copies, waits for them, and re-layouts: 3.04 us -> none
    pallas_call x0 -> x1, Pallas kernels: none -> 1.88 us  [gathered_shards(): pl.pallas_call(finish_kernel, out_shape=(jax.ShapeDtypeStruct((1, local),...]
    pallas_call x1, Pallas kernels: 31.6 us -> 30.2 us  [gathered_shards(): pl.pallas_call(functools.partial(embed_kernel, n_rows, n_cents), out_shap...]
where the time goes in v3:
time: 33 us; the launch traced here: 32.7 us
  Pallas kernels  32.1 us (97%)
  between operations  0.64 us (2%)
    pallas_call x1, Pallas kernels, gathered_shards(): pl.pallas_call(functools.partial(embed_kernel, n_rows, n_cents), out_shap...  30.2 us
    pallas_call x1, Pallas kernels, gathered_shards(): pl.pallas_call(finish_kernel, out_shape=(jax.ShapeDtypeStruct((1, local),...  1.88 us

profile of v3, /device:TPU:0, one launch (start us, length us, event | category | flops | bytes accessed | tf_op | source)
XLA Modules:
  0.0 32.7 jit_solution(12913443191919886468)
XLA Ops:
  0.6 30.2 %shard_map.68 = (f32[1,64]{1,0:T(1,128)}, f32[1024,128]{1,0:T(8,128)}) custom-call(bf16[64,128]{1,0:T(8,128)(2,1)} %emb_hbm.1, s32[1,64]{1,0:T(1,128)} %bitcast.4, f32[128,128]{1,0:T(8,128)} %rotation_hbm.1, f32[1024,128]{1,0:T(8,128)} %offset_hbm.1, s32[1,1024]{1,0:T(1,128)} %bitcast.3), custom_call_target="tpu_custom_call" | custom-call | tf_op jit(solution)/shard_map/pallas_call | solution.py:388
  30.8 1.9 %shard_map.69 = (f32[1,64]{1,0:T(1,128)}, f32[1024,128]{1,0:T(8,128)}) custom-call(f32[1,64]{1,0:T(1,128)} %get-tuple-element.6.energy_in, f32[1024,128]{1,0:T(8,128)} %get-tuple-element.7.center_in), custom_call_target="tpu_custom_call" | custom-call | tf_op jit(solution)/shard_map/pallas_call | solution.py:420
